TPU v7x, 32 devices: a whole 2x2x4 slice. The times are simulated.
32 devices in a mesh: groups: 2 (over y), prow: 4 (over x, core), pcol: 4 (over z).
Axes of the slice: x: 2, y: 2, z: 4, core: 2. Of those that a mesh axis runs over, the one named last changes fastest.
Arguments:
- anc_inverse: float32 [4096, 2048], P(('groups', 'prow'), 'pcol'), parts along dimension 0
- anc_factor: float32 [8, 2048, 256], P('groups', ('prow', 'pcol')), parts along dimension 0, may hold values from -0.0625 to 0.0625
- win_factor: float32 [12, 256, 256], P('groups'), parts along dimension 0, may hold values from -0.1875 to 0.1875
- diag_inverse: float32 [8, 256, 256], P('groups'), parts along dimension 0
- first_reader: int32 [32], P('groups'), parts along dimension 0, may hold values from 0 to 4
Outputs:
- anc_panels: float32 [8, 2048, 256], P('groups', ('prow', 'pcol')), parts along dimension 0
- window_inverse: float32 [8, 4, 256, 256], P('groups'), parts along dimension 0
There are 2 independent parts, one for each index of `groups`. A program takes and returns all parts, laid end to end along the dimension named above; each array names one. Nothing has to cross between parts.
Inputs may be any that keep to these rules, and one draw needn't show every extreme that they name: Ancestor block b belongs to the pattern of supernode k exactly when first_reader[b] <= k; the value 4 puts it in no pattern, so patterns grow with k. Within each part, anc_inverse is symmetric: anc_inverse[r, s] = anc_inverse[s, r].
All inputs are finite; a program needn't handle non-finite values.
Results may differ from a plain program's by a relative error of at most 0.0003.
Values sent between devices are 32-bit elements; how exact they have to be, the bound alone decides.
A program may use at most 64 MiB of HBM per device.

v0:
```python
import jax
import jax.numpy as jnp
from jax import lax
from jax.sharding import PartitionSpec as P

BLK = 128


def broadcast(array, axis, root):
    mine = lax.axis_index(axis) == root
    return lax.psum(jnp.where(mine, array, jnp.zeros_like(array)), axis)


def to_columns(stacked, per_column, pcol_at):
    gathered = lax.all_gather(stacked, "pcol", axis=1, tiled=True)
    pieces = [
        broadcast(gathered, "prow", pcol_at * per_column + offset) for offset in range(per_column)
    ]
    return jnp.concatenate(pieces, axis=1)


def window_algebra(summed, upper_all, diag_inverse, window_count):
    highest = lax.Precision.HIGHEST
    blocks = [[None] * window_count for column in range(window_count)]
    for node in reversed(range(window_count)):
        linv = diag_inverse[node]
        later = list(range(node + 1, window_count))
        upper_u = upper_all[node]
        cross = {}
        for position, other in enumerate(later):
            term = summed[node][position]
            for second in later:
                term = term + jnp.dot(blocks[other][second], upper_u[second], precision=highest)
            cross[other] = term
        own = jnp.dot(linv.T, linv, precision=highest) + summed[node][len(later)]
        for other in later:
            own = own + jnp.dot(upper_u[other].T, cross[other], precision=highest)
        blocks[node][node] = own
        for other in later:
            blocks[other][node] = -cross[other]
            blocks[node][other] = -cross[other].T
    return jnp.stack([jnp.stack(blocks[row_at]) for row_at in range(window_count)])


def per_device(anc_inverse, anc_factor, win_factor, diag_inverse, first_reader):
    highest = lax.Precision.HIGHEST
    n_prow = lax.axis_size("prow")
    n_pcol = lax.axis_size("pcol")
    per_column = n_prow // n_pcol
    prow_at = lax.axis_index("prow")
    pcol_at = lax.axis_index("pcol")
    window_count = diag_inverse.shape[0]
    fine_rows = anc_factor.shape[1]
    start_row = (prow_at * n_pcol + pcol_at) * fine_rows
    block_of = (start_row + jnp.arange(fine_rows, dtype=jnp.int32)) // BLK
    block_ids = jnp.arange(first_reader.shape[0], dtype=jnp.int32)
    readers = jnp.sum(
        jnp.where(block_of[:, None] == block_ids[None, :], first_reader[None, :], 0), axis=1
    )
    row_masks = [(readers <= node).astype(jnp.float32)[:, None] for node in range(window_count)]
    lower_all = [
        jnp.dot(anc_factor[node], diag_inverse[node], precision=highest) * row_masks[node]
        for node in range(window_count)
    ]
    whole = to_columns(jnp.stack(lower_all), per_column, pcol_at)
    column_panels = [whole[node] for node in range(window_count)]
    panels = [None] * window_count
    upper_all = [None] * window_count
    summed = [None] * window_count
    for node in reversed(range(window_count)):
        linv = diag_inverse[node]
        later = list(range(node + 1, window_count))
        upper_u = {}
        for other in later:
            upper_u[other] = jnp.dot(
                win_factor[other * (other - 1) // 2 + node], linv, precision=highest
            )
        upper_all[node] = upper_u
        columns = column_panels[node]
        full_x = lax.psum_scatter(
            jnp.dot(anc_inverse, columns, precision=highest),
            "pcol",
            scatter_dimension=0,
            tiled=True,
        )
        for other in later:
            full_x = full_x + jnp.dot(panels[other], upper_u[other], precision=highest)
        partials = [jnp.dot(panels[other].T, lower_all[node], precision=highest) for other in later]
        partials.append(jnp.dot(lower_all[node].T, full_x, precision=highest))
        panels[node] = -full_x * row_masks[node]
        summed[node] = list(lax.psum(tuple(partials), ("prow", "pcol")))
    window_inverse = window_algebra(summed, upper_all, diag_inverse, window_count)
    return (jnp.stack(panels), window_inverse)


def solution(mesh):
    return jax.shard_map(
        per_device,
        mesh=mesh,
        in_specs=(
            P(("groups", "prow"), "pcol"),
            P("groups", ("prow", "pcol"), None),
            P("groups", None, None),
            P("groups", None, None),
            P("groups"),
        ),
        out_specs=(P("groups", ("prow", "pcol"), None), P("groups", None, None, None)),
        check_vma=False,
    )
```

profile of v0, /device:TPU:0, one launch (start us, length us, event | category | flops | bytes accessed | tf_op | source)
XLA Modules:
  0.0 358.3 jit_solution(12927005311065160913)
XLA Ops:
  10.8 1.3 convolution_multiply_fusion.1
  14.4 48.7 %all-gather.2.cloned.1.call-done = f32[4,512,256]{2,1,0:T(8,128)} async-done(((f32[4,128,256]{2,1,0:T(8,128)}), f32[4,512,256]{2,1,0:T(8,128)}) %all-gather.2.cloned.1.call-update) | async-done | bytes 2097168 | tf_op jit(solution)/shard_map/all_gather | solution.py:15
  63.2 3.1 broadcast_select_fusion
  66.3 50.1 %all-reduce.4.cloned.1.call-done = f32[4,512,256]{2,1,0:T(8,128)} async-done(((f32[4,512,256]{2,1,0:T(8,128)}), f32[4,512,256]{2,1,0:T(8,128)}) %all-reduce.4.cloned.1.call-update) | async-done | bytes 2097168 | tf_op jit(solution)/shard_map/psum | solution.py:11
  116.4 2.8 convolution_bitcast_fusion
  119.4 2.9 convolution_bitcast_fusion.1
  125.0 2.9 convolution_bitcast_fusion.2
  132.0 2.1 fusion.11
  134.1 2.9 convolution_bitcast_fusion.3
  137.2 4.0 %reduce-scatter.11.cloned.1.call-done = f32[128,256]{1,0:T(8,128)} async-done(((f32[512,256]{1,0:T(8,128)}), f32[128,256]{1,0:T(8,128)}) %reduce-scatter.11.cloned.1.call-update) | async-done | bytes 131088 | tf_op jit(solution)/shard_map/reduce_scatter | solution.py:80
  141.2 22.7 %reduce-scatter.9.cloned.1.call-done = f32[128,256]{1,0:T(8,128)} async-done(((f32[512,256]{1,0:T(8,128)}), f32[128,256]{1,0:T(8,128)}) %reduce-scatter.9.cloned.1.call-update) | async-done | bytes 131088 | tf_op jit(solution)/shard_map/reduce_scatter | solution.py:80
  163.9 1.4 convolution_add_fusion.29
  165.3 20.7 %reduce-scatter.7.cloned.1.call-done = f32[128,256]{1,0:T(8,128)} async-done(((f32[512,256]{1,0:T(8,128)}), f32[128,256]{1,0:T(8,128)}) %reduce-scatter.7.cloned.1.call-update) | async-done | bytes 131088 | tf_op jit(solution)/shard_map/reduce_scatter | solution.py:80
  188.5 2.2 fusion.80
  190.7 2.0 fusion.79
  192.7 2.1 fusion.66
  194.8 2.1 fusion.65
  198.0 10.0 %reduce-scatter.5.cloned.1.call-done = f32[128,256]{1,0:T(8,128)} async-done(((f32[512,256]{1,0:T(8,128)}), f32[128,256]{1,0:T(8,128)}) %reduce-scatter.5.cloned.1.call-update) | async-done | bytes 131088 | tf_op jit(solution)/shard_map/reduce_scatter | solution.py:80
  211.0 2.1 fusion.78
  220.8 99.6 %all-reduce.6.cloned.1.call-done = (f32[256,256]{1,0:T(8,128)}, f32[256,256]{1,0:T(8,128)}, f32[256,256]{0,1:T(8,128)}, f32[256,256]{1,0:T(8,128)}, f32[256,256]...) async-done(((f32[256,256]{1,0:T(8,128)}, f32[256,256]{1,0:T(8,128)}, ...) | async-done | bytes 2621456 | tf_op jit(solution)/shard_map/psum | solution.py:91
  320.3 1.5 convolution_add_fusion.20
  321.9 1.5 convolution_add_fusion.19
  323.4 1.5 convolution_add_fusion.14
  349.0 2.4 pad_maximum_fusion
  (147 shorter events, 50.8 us)
Async XLA Ops:
  7.2 109.3 %copy-start = (f32[512,512]{1,0:T(8,128)S(1)}, f32[512,512]{1,0:T(8,128)}, u32[]{:S(2)}) copy-start(f32[512,512]{1,0:T(8,128)} %param.5) | copy-start | bytes 3145732
  7.2 56.0 %all-gather.2.cloned.1.call-start = ((), (), s32[]{:S(2)}) async-start(), calls=%async_computation.4 | async-start | bytes 2621440 | tf_op jit(solution)/shard_map/all_gather | solution.py:15
  9.4 56.9 %copy-start.6 = (f32[128,256]{1,0:T(8,128)}, f32[128,256]{1,0:T(8,128)S(1)}, u32[]{:S(2)}) copy-start(f32[128,256]{1,0:T(8,128)S(1)} %convolution_multiply_fusion.3) | copy-start | bytes 393220
  10.7 55.5 %copy-start.13 = (f32[128,256]{1,0:T(8,128)}, f32[128,256]{1,0:T(8,128)S(1)}, u32[]{:S(2)}) copy-start(f32[128,256]{1,0:T(8,128)S(1)} %convolution_multiply_fusion.2) | copy-start | bytes 393220
  12.1 54.1 %copy-start.17 = (f32[128,256]{1,0:T(8,128)}, f32[128,256]{1,0:T(8,128)S(1)}, u32[]{:S(2)}) copy-start(f32[128,256]{1,0:T(8,128)S(1)} %convolution_multiply_fusion.1) | copy-start | bytes 393220
  13.5 52.8 %copy-start.19 = (f32[128,256]{1,0:T(8,128)}, f32[128,256]{1,0:T(8,128)S(1)}, u32[]{:S(2)}) copy-start(f32[128,256]{1,0:T(8,128)S(1)} %convolution_multiply_fusion) | copy-start | bytes 393220
  14.4 102.1 %all-reduce.4.cloned.1.call-start = ((), (), s32[]{:S(2)}) async-start(), calls=%async_computation.5 | async-start | bytes 4194304 | tf_op jit(solution)/shard_map/psum | solution.py:11
  66.3 74.9 %reduce-scatter.11.cloned.1.call-start = ((), (), s32[]{:S(2)}) async-start(), calls=%async_computation.9 | async-start | bytes 655360 | tf_op jit(solution)/shard_map/reduce_scatter | solution.py:80
  119.3 44.6 %reduce-scatter.9.cloned.1.call-start = ((), (), s32[]{:S(2)}) async-start(), calls=%async_computation.8 | async-start | bytes 655360 | tf_op jit(solution)/shard_map/reduce_scatter | solution.py:80
  122.3 63.7 %reduce-scatter.7.cloned.1.call-start = ((), (), s32[]{:S(2)}) async-start(), calls=%async_computation.7 | async-start | bytes 655360 | tf_op jit(solution)/shard_map/reduce_scatter | solution.py:80
  127.9 80.1 %reduce-scatter.5.cloned.1.call-start = ((), (), s32[]{:S(2)}) async-start(), calls=%async_computation.6 | async-start | bytes 655360 | tf_op jit(solution)/shard_map/reduce_scatter | solution.py:80
  137.0 183.4 %all-reduce.6.cloned.1.call-start = ((), (), s32[]{:S(2)}) async-start(), calls=%async_computation.10 | async-start | bytes 5242880 | tf_op jit(solution)/shard_map/psum | solution.py:91
  165.2 22.0 %copy-start.5 = (f32[128,256]{1,0:T(8,128)}, f32[128,256]{1,0:T(8,128)S(1)}, u32[]{:S(2)}) copy-start(f32[128,256]{1,0:T(8,128)S(1)} %convolution_add_fusion.29) | copy-start | bytes 393220
  186.0 6.7 %copy-start.14 = (f32[128,256]{1,0:T(8,128)S(1)}, f32[128,256]{1,0:T(8,128)}, u32[]{:S(2)}) copy-start(f32[128,256]{1,0:T(8,128)} %copy-done.13) | copy-start | bytes 393220
  186.0 8.8 %copy-start.7 = (f32[128,256]{1,0:T(8,128)S(1)}, f32[128,256]{1,0:T(8,128)}, u32[]{:S(2)}) copy-start(f32[128,256]{1,0:T(8,128)} %copy-done.6) | copy-start | bytes 393220
  188.5 8.4 %copy-start.16 = (f32[128,256]{1,0:T(8,128)}, f32[128,256]{1,0:T(8,128)S(1)}, u32[]{:S(2)}) copy-start(f32[128,256]{1,0:T(8,128)S(1)} %convolution_add_fusion.27) | copy-start | bytes 393220
  188.5 22.2 %copy-start.2 = (f32[128,256]{1,0:T(8,128)S(1)}, f32[128,256]{1,0:T(8,128)}, u32[]{:S(2)}) copy-start(f32[128,256]{1,0:T(8,128)} %reduce-scatter.11.cloned.1.call-done) | copy-start | bytes 393220
  208.1 5.0 %copy-start.20 = (f32[128,256]{1,0:T(8,128)S(1)}, f32[128,256]{1,0:T(8,128)}, u32[]{:S(2)}) copy-start(f32[128,256]{1,0:T(8,128)} %copy-done.19) | copy-start | bytes 393220
  208.1 6.1 %copy-start.18 = (f32[128,256]{1,0:T(8,128)S(1)}, f32[128,256]{1,0:T(8,128)}, u32[]{:S(2)}) copy-start(f32[128,256]{1,0:T(8,128)} %copy-done.17) | copy-start | bytes 393220
  208.1 7.3 %copy-start.15 = (f32[128,256]{1,0:T(8,128)S(1)}, f32[128,256]{1,0:T(8,128)}, u32[]{:S(2)}) copy-start(f32[128,256]{1,0:T(8,128)} %copy-done.13) | copy-start | bytes 393220
  208.1 8.5 %copy-start.8 = (f32[128,256]{1,0:T(8,128)S(1)}, f32[128,256]{1,0:T(8,128)}, u32[]{:S(2)}) copy-start(f32[128,256]{1,0:T(8,128)} %copy-done.6) | copy-start | bytes 393220
  211.0 5.6 %copy-start.21 = (f32[128,256]{1,0:T(8,128)}, f32[128,256]{1,0:T(8,128)S(1)}, u32[]{:S(2)}) copy-start(f32[128,256]{1,0:T(8,128)S(1)} %convolution_add_fusion.24) | copy-start | bytes 393220
  321.9 5.6 %copy-start.3 = (f32[256,256]{1,0:T(8,128)}, f32[256,256]{1,0:T(8,128)S(1)}, u32[]{:S(2)}) copy-start(f32[256,256]{1,0:T(8,128)S(1)} %convolution_add_fusion.20) | copy-start | bytes 786436
  339.0 4.8 %copy-start.12 = (f32[256,256]{0,1:T(8,128)S(1)}, f32[256,256]{0,1:T(8,128)}, u32[]{:S(2)}) copy-start(f32[256,256]{0,1:T(8,128)} %copy-done.11) | copy-start | bytes 786436
  (20 other events, 45.0 us)
Sparse Core Ops, SparseCore 0:
  14.5 48.6 all-gather.1
  66.4 49.9 all-reduce.3
  119.4 21.7 reduce-scatter.10
  144.0 19.8 reduce-scatter.8
  166.1 19.8 reduce-scatter.6
  188.2 19.8 reduce-scatter.4
  217.9 102.3 all-reduce.5
where the time goes:
time: 359 us; the launch traced here: 358 us
  waiting for transfers between devices  256 us (71%)
  matrix products  65.6 us (18%)
  other arithmetic  16.4 us (5%)
  between operations  14.9 us (4%)
  local copies, waits for them, and re-layouts  5.02 us (1%)
    psum x1, waiting for transfers between devices, per_device(): summed[node] = list(lax.psum(tuple(partials), ('prow', 'pcol')))  99.6 us
    reduce_scatter x4, waiting for transfers between devices, per_device(): lax.psum_scatter(jnp.dot(anc_inverse, columns, precision=highest), 'pcol'...  57.4 us
    psum x1, waiting for transfers between devices, broadcast(): return lax.psum(jnp.where(mine, array, jnp.zeros_like(array)), axis)  50.1 us
    all_gather x1, waiting for transfers between devices, to_columns(): gathered = lax.all_gather(stacked, 'pcol', axis=1, tiled=True)  48.7 us
    dot_general x4, matrix products, per_device(): jnp.dot(anc_inverse, columns, precision=highest)  11.5 us
    dot_general x14, matrix products, window_algebra(): jnp.dot(blocks[other][second], upper_u[second], precision=highest)  9.39 us
    dot_general x6, matrix products, per_device(): jnp.dot(panels[other].T, lower_all[node], precision=highest)  8.88 us
    dot_general x6, matrix products, per_device(): jnp.dot(win_factor[other * (other - 1) // 2 + node], linv, precision=high...  8.71 us
  transfers between devices with their start and end apart: 7, of which 7 were waited for; matrix products, arithmetic and copies ran while one was open for 9% of the time, Pallas kernels for 0%

commit v1 on v0

v1 whole, which is shorter than its diff:
```python
import functools

import jax
import jax.numpy as jnp
from jax import lax
from jax.experimental import pallas as pl
from jax.experimental.pallas import tpu as pltpu
from jax.sharding import PartitionSpec as P

BLK = 128
PIECES = 4
MESH = pl.DeviceIdType.MESH


def split(x):
    high = x.astype(jnp.bfloat16)
    return high, (x - high.astype(jnp.float32)).astype(jnp.bfloat16)


def product(a, b):
    dot = functools.partial(jnp.dot, preferred_element_type=jnp.float32)
    return dot(a[0], b[0]) + (dot(a[0], b[1]) + dot(a[1], b[0]))


def matmul(a, b):
    return product(split(a), split(b))


def pair_at(first, second):
    return second * (second + 1) // 2 + first


def kernel(
    n_prow, n_pcol, readers_ref, a_ref, f_ref, win_ref, diag_ref, panels_ref, z_ref,
    v_ref, whole_ref, part_ref, inbox_ref, g1_send, g1_recv, g2_send, g2_recv, rs_send, rs_recv,
):
    count, fine, width = f_ref.shape
    per_column = n_prow // n_pcol
    step = n_prow // PIECES
    quarter = fine // PIECES
    p = lax.axis_index("prow")
    z = lax.axis_index("pcol")
    order = list(reversed(range(count)))

    barrier = pltpu.get_barrier_semaphore()

    def greet(at, carry):
        row, col = at // n_pcol, at % n_pcol

        @pl.when(at != p * n_pcol + z)
        def _():
            pl.semaphore_signal(barrier, inc=1, device_id={"prow": row, "pcol": col}, device_id_type=MESH)

        return carry

    lax.fori_loop(0, n_prow * n_pcol, greet, 0)

    reader = readers_ref[(p * n_pcol + z) * fine // BLK]
    masks = [jnp.where(reader <= node, 1.0, 0.0).astype(jnp.float32) for node in range(count)]

    def local_v(node):
        total = f_ref[node] * masks[node]
        for other in range(node + 1, count):
            total = total - matmul(v_ref[other], win_ref[other * (other - 1) // 2 + node])
        v_ref[node] = matmul(total, diag_ref[node])

    source = (p % per_column) * n_pcol + z
    column = p // per_column

    def g1_copy(node, q):
        return pltpu.make_async_remote_copy(
            src_ref=v_ref.at[node, pl.ds(q * quarter, quarter)],
            dst_ref=whole_ref.at[node, source, q],
            send_sem=g1_send.at[node, q],
            recv_sem=g1_recv.at[node],
            device_id={"prow": q * step, "pcol": column},
            device_id_type=MESH,
        )

    def g1_start(node):
        for q in range(PIECES):
            mine = jnp.logical_and(p == q * step, z == column)

            @pl.when(mine)
            def _():
                pltpu.make_async_copy(
                    v_ref.at[node, pl.ds(q * quarter, quarter)],
                    whole_ref.at[node, source, q],
                    g1_recv.at[node],
                ).start()

            @pl.when(jnp.logical_not(mine))
            def _():
                g1_copy(node, q).start()

    def g1_finish(node):
        for q in range(PIECES):
            mine = jnp.logical_and(p == q * step, z == column)

            @pl.when(jnp.logical_not(mine))
            def _():
                g1_copy(node, q).wait_send()

    def g2_copy(node, q, row):
        return pltpu.make_async_remote_copy(
            src_ref=whole_ref.at[node, :, q],
            dst_ref=whole_ref.at[node, :, q],
            send_sem=g2_send.at[node, row],
            recv_sem=g2_recv.at[node, q],
            device_id={"prow": row, "pcol": z},
            device_id_type=MESH,
        )

    def g2_start(node):
        for q in range(PIECES):
            @pl.when(p == q * step)
            def _():
                held = whole_ref.at[node, :, q]
                pltpu.make_async_copy(held, held, g1_recv.at[node]).wait()
                for row in range(n_prow):
                    if row != q * step:
                        g2_copy(node, q, row).start()

    def g2_wait(node):
        for q in range(PIECES):
            @pl.when(p != q * step)
            def _():
                g2_copy(node, q, 0).wait_recv()

    def g2_finish(node):
        for q in range(PIECES):
            @pl.when(p == q * step)
            def _():
                for row in range(n_prow):
                    if row != q * step:
                        g2_copy(node, q, row).wait_send()

    def rs_copy(node, side, dest):
        return pltpu.make_async_remote_copy(
            src_ref=part_ref.at[node, dest],
            dst_ref=inbox_ref.at[node, side, dest],
            send_sem=rs_send.at[node, dest],
            recv_sem=rs_recv.at[node, side, dest],
            device_id={"prow": p, "pcol": z + 1 if side == 0 else z - 1},
            device_id_type=MESH,
        )

    def rs_steps(node, relayed):
        for far in range(1, n_pcol):
            for side in (0, 1):
                dest = n_pcol - far if side == 0 else far - 1
                first = z == (0 if side == 0 else n_pcol - 1)
                before = z < dest if side == 0 else z > dest
                if relayed:
                    @pl.when(jnp.logical_and(before, jnp.logical_not(first)))
                    def _():
                        rs_copy(node, side, dest).wait_recv()
                        part_ref[node, dest] += inbox_ref[node, side, dest]
                        rs_copy(node, side, dest).start()
                else:
                    @pl.when(jnp.logical_and(before, first))
                    def _():
                        rs_copy(node, side, dest).start()

    def rs_end(node):
        for dest in range(n_pcol):
            @pl.when(z == dest)
            def _():
                total = part_ref[node, dest]
                if dest > 0:
                    rs_copy(node, 0, dest).wait_recv()
                    total = total + inbox_ref[node, 0, dest]
                if dest < n_pcol - 1:
                    rs_copy(node, 1, dest).wait_recv()
                    total = total + inbox_ref[node, 1, dest]
                part_ref[node, dest] = total
                panels_ref[node] = -total * masks[node]

    def rs_finish(node):
        for dest in range(n_pcol):
            @pl.when(z != dest)
            def _():
                rs_copy(node, 0, dest).wait_send()

    a_split = []

    def multiply(node):
        rows = a_ref.shape[0]
        gathered = whole_ref[node].reshape(a_ref.shape[1], width)
        result = product(a_split[0], split(gathered))
        part_ref[node] = result.reshape(n_pcol, fine, width)

    vt_split = {}

    def window_part(node):
        x = split(-panels_x(node))
        for other in range(node + 1):
            z_ref[pair_at(other, node)] = product(vt_split[other], x)

    def panels_x(node):
        return -part_ref[node, z]

    local_v(order[0])
    pl.semaphore_wait(barrier, n_prow * n_pcol - 1)
    g1_start(order[0])
    for node in order[1:]:
        local_v(node)
        g1_start(node)
    a_split.append(split(a_ref[...]))
    for node in range(count):
        vt_split[node] = split(v_ref[node].T)
    g2_start(order[0])
    for at, node in enumerate(order):
        if at + 1 < count:
            g2_start(order[at + 1])
        g2_wait(node)
        multiply(node)
        rs_steps(node, False)
        if at >= 1:
            rs_steps(order[at - 1], True)
        if at >= 2:
            rs_end(order[at - 2])
            window_part(order[at - 2])
    rs_steps(order[-1], True)
    for node in order[max(count - 2, 0):]:
        rs_end(node)
        window_part(node)
    for node in order:
        g1_finish(node)
        g2_finish(node)
        rs_finish(node)


def sweep(n_prow, n_pcol, readers, anc_inverse, anc_factor, win_factor, diag_inverse):
    count, fine, width = anc_factor.shape
    pairs = count * (count + 1) // 2
    sources = n_prow // n_pcol * n_pcol
    vmem = pl.BlockSpec(memory_space=pltpu.VMEM)
    return pl.pallas_call(
        functools.partial(kernel, n_prow, n_pcol),
        out_shape=(
            jax.ShapeDtypeStruct((count, fine, width), jnp.float32),
            jax.ShapeDtypeStruct((pairs, width, width), jnp.float32),
        ),
        in_specs=[pl.BlockSpec(memory_space=pltpu.SMEM)] + [vmem] * 4,
        out_specs=(vmem, vmem),
        scratch_shapes=[
            pltpu.VMEM((count, fine, width), jnp.float32),
            pltpu.VMEM((count, sources, PIECES, fine // PIECES, width), jnp.float32),
            pltpu.VMEM((count, n_pcol, fine, width), jnp.float32),
            pltpu.VMEM((count, 2, n_pcol, fine, width), jnp.float32),
            pltpu.SemaphoreType.DMA((count, PIECES)),
            pltpu.SemaphoreType.DMA((count,)),
            pltpu.SemaphoreType.DMA((count, n_prow)),
            pltpu.SemaphoreType.DMA((count, PIECES)),
            pltpu.SemaphoreType.DMA((count, n_pcol)),
            pltpu.SemaphoreType.DMA((count, 2, n_pcol)),
        ],
        compiler_params=pltpu.CompilerParams(
            collective_id=0, has_side_effects=True, vmem_limit_bytes=48 * 2**20
        ),
    )(readers, anc_inverse, anc_factor, win_factor, diag_inverse)


def window_own(win_factor, diag_inverse):
    dot = functools.partial(jnp.dot, precision=lax.Precision.HIGH)
    count, width, _ = diag_inverse.shape
    columns = []
    for node in range(count):
        column = [jnp.zeros((width, width), jnp.float32)] * node + [diag_inverse[node]]
        for row in range(node + 1, count):
            total = sum(dot(win_factor[row * (row - 1) // 2 + at], column[at]) for at in range(node, row))
            column.append(-dot(diag_inverse[row], total))
        columns.append(jnp.concatenate(column, axis=0))
    whole = jnp.concatenate(columns, axis=1)
    return dot(whole.T, whole)


def per_device(anc_inverse, anc_factor, win_factor, diag_inverse, first_reader):
    n_prow = lax.axis_size("prow")
    n_pcol = lax.axis_size("pcol")
    count, _, width = anc_factor.shape
    panels, partial = sweep(
        n_prow, n_pcol, first_reader, anc_inverse, anc_factor, win_factor, diag_inverse
    )
    own = window_own(win_factor, diag_inverse)
    summed = lax.psum(partial, ("prow", "pcol"))
    own = own.reshape(count, width, count, width).transpose(0, 2, 1, 3)
    cross = jnp.stack([
        jnp.stack([
            summed[pair_at(row, col)] if row <= col else summed[pair_at(col, row)].T
            for col in range(count)
        ])
        for row in range(count)
    ])
    return panels, own + cross


def solution(mesh):
    return jax.shard_map(
        per_device,
        mesh=mesh,
        in_specs=(
            P(("groups", "prow"), "pcol"),
            P("groups", ("prow", "pcol"), None),
            P("groups", None, None),
            P("groups", None, None),
            P("groups"),
        ),
        out_specs=(P("groups", ("prow", "pcol"), None), P("groups", None, None, None)),
        check_vma=False,
    )
```

time: 359 us -> 215 us (0.60)
  waiting for transfers between devices: 256 us -> 78.8 us
  Pallas kernels: 0 us -> 82 us
  matrix products: 65.6 us -> 15.1 us
  local copies, waits for them, and re-layouts: 5.02 us -> 17.4 us
  other arithmetic: 16.4 us -> 7.05 us
    pallas_call x0 -> x1, Pallas kernels: none -> 82 us  [sweep(): pl.pallas_call(functools.partial(kernel, n_prow, n_pcol), out_shape=(jax....]
    psum x2 -> x1, waiting for transfers between devices: 150 us -> 78.7 us  [per_device(): summed = lax.psum(partial, ('prow', 'pcol'))]
    reduce_scatter x4 -> x0, waiting for transfers between devices: 57.4 us -> none  [per_device(): lax.psum_scatter(jnp.dot(anc_inverse, columns, precision=highest), 'pcol'...]
    dot_general x54 -> x17, matrix products: 65.6 us -> 15.1 us  [the longest x1 10 us: window_own(): return dot(whole.T, whole)]
    all_gather x1 -> x0, waiting for transfers between devices: 48.7 us -> none  [to_columns(): gathered = lax.all_gather(stacked, 'pcol', axis=1, tiled=True)]
    another operation x14 -> x3, other arithmetic: 12.5 us -> 3.97 us  [per_device(): jnp.stack([jnp.stack([summed[pair_at(row, col)] if row <= col else summed...]
    reshape x0 -> x1, local copies, waits for them, and re-layouts: none -> 5.67 us  [per_device(): own = own.reshape(count, width, count, width).transpose(0, 2, 1, 3)]
    unnamed x74 -> x25, local copies, waits for them, and re-layouts: 1.21 us -> 6.87 us
  transfers between devices with their start and end apart: 7 -> 1, of which waited for: 7 -> 1; matrix products, arithmetic and copies ran while one was open for 9% -> 10% of each run, Pallas kernels for 0% -> 0%
where the time goes in v1:
time: 215 us
  Pallas kernels  82 us (38%)
  waiting for transfers between devices  78.8 us (37%)
  local copies, waits for them, and re-layouts  17.4 us (8%)
  matrix products  15.1 us (7%)
  between operations  14.3 us (7%)
  other arithmetic  7.05 us (3%)
    pallas_call x1, Pallas kernels, sweep(): pl.pallas_call(functools.partial(kernel, n_prow, n_pcol), out_shape=(jax....  82 us
    psum x1, waiting for transfers between devices, per_device(): summed = lax.psum(partial, ('prow', 'pcol'))  78.7 us
    dot_general x1, matrix products, window_own(): return dot(whole.T, whole)  10 us
    unnamed x25, local copies, waits for them, and re-layouts  6.87 us
    reshape x1, local copies, waits for them, and re-layouts, per_device(): own = own.reshape(count, width, count, width).transpose(0, 2, 1, 3)  5.67 us
  transfers between devices with their start and end apart: 1, of which 1 were waited for; matrix products, arithmetic and copies ran while one was open for 10% of the time, Pallas kernels for 0%

profile of v1, /device:TPU:0, one launch (start us, length us, event | category | flops | bytes accessed | tf_op | source)
XLA Modules:
  0.0 214.7 jit_solution(12225511668491164409)
XLA Ops:
  7.2 1.2 copy-done
  8.4 1.4 copy-done.2
  9.8 1.2 copy-done.4
  11.1 1.0 copy-done.5
  12.1 0.7 copy-done.6
  12.8 82.0 %shard_map.68 = (f32[4,128,256]{2,1,0:T(8,128)S(1)}, f32[10,256,256]{2,1,0:T(8,128)}) custom-call(s32[16]{0:T(128)S(1)} %copy-done.6, f32[512,512]{1,0:T(8,128)S(1)} %copy-done.4, f32[4,128,256]{2,1,0:T(8,128)S(1)} %copy-done.5, f32[6,256,256]{2,1,0:T(8,128)S(1)} %copy-done.2, f32[4,256,256]{2,1,0:T(8,128)S(1)} %copy-done), custom_call_target="tpu_custom_call" | custom-call | tf_op jit(solution)/shard_map/pallas_call | solution.py:239
  96.8 0.3 convolution_negate_fusion.2
  97.0 0.3 fusion.27
  97.3 1.0 fusion.26
  98.3 0.3 convolution_negate_fusion.5
  98.6 0.3 fusion.30
  98.9 0.3 fusion.31
  100.2 10.0 %fusion = f32[1024,1024]{1,0:T(8,128)} fusion(f32[256,256]{1,0:T(8,128)S(1)} %get-tuple-element.19, f32[256,256]{1,0:T(8,128)S(1)} %fusion.25, f32[256,256]{1,0:T(8,128)S(1)} %get-tuple-element.20, f32[512,256]{1,0:T(8,128)S(1)} %concatenate.21, f32[256,256]{1,0:T(8,128)} %fusion.26, f32[256,256]{1,0:T(8,128)S(1)} %bitcast.128, ...), kind=kOutput, calls=%fused_computation.1 | convolution fusion | flops 6456082432 | bytes 7602176 | tf_op jit(solution)/shard_map/dot_general | solution.py:276
  110.2 5.7 %reshape.7 = f32[4,256,4,256]{3,2,1,0:T(4,128)} reshape(f32[1024,1024]{1,0:T(8,128)} %fusion) | data formatting | bytes 8388608 | tf_op jit(solution)/shard_map/reshape | solution.py:288
  115.9 78.7 %all-reduce.3.cloned.1.call-done = f32[10,256,256]{2,1,0:T(8,128)} async-done(((f32[10,256,256]{2,1,0:T(8,128)}), f32[10,256,256]{2,1,0:T(8,128)}) %all-reduce.3.cloned.1.call-update) | async-done | bytes 2621456 | tf_op jit(solution)/shard_map/psum | solution.py:287
  194.6 2.7 %fusion.61 = (f32[1,256,256]{2,1,0:T(8,128)}, f32[1,256,256]{1,2,0:T(8,128)S(1)}, f32[1,256,256]{1,2,0:T(8,128)S(1)}, f32[1,256,256]{2,1,0:T(8,128)S(1)}, f32[1,...) fusion(f32[10,256,256]{2,1,0:T(8,128)} %all-reduce.3.cloned.1.c, ...), kind=kLoop, calls=%fused_computation.85 | loop fusion | bytes 5242880 | tf_op jit(solution)/shard_map/slice | solution.py:291
  197.7 0.8 copy.21
  198.5 0.9 copy.22
  199.5 1.0 maximum_bitcast_fusion.1
  200.6 0.3 copy.23
  201.1 1.4 maximum_bitcast_fusion.3
  202.5 1.5 maximum_bitcast_fusion
  204.0 3.1 %maximum_add_fusion = f32[4,4,256,256]{3,2,1,0:T(8,128)} fusion(f32[1,4,256,256]{3,2,1,0:T(8,128)S(1)} %maximum_bitcast_fusion.3, f32[1,4,256,256]{3,2,1,0:T(8,128)S(1)} %get-tuple-element.22, f32[1,4,256,256]{3,2,1,0:T(8,128)S(1)} %copy.23, f32[1,4,256,256]{3,2,1,0:T(8,128)S(1)} %get-tuple-element.21, f32[4,256,4,256]{3,2,1,0:T(4,128)S(1)} %copy-done.7), kind=kLoop, calls=%fused_computation.25 | loop fusion | flops 4194304 | bytes 12582912 | tf_op jit(solution)/shard_map/add | solution.py:296
  207.1 0.8 copy.31
  (36 shorter events, 3.5 us)
Async XLA Ops:
  7.2 187.5 %all-reduce.3.cloned.1.call-start = ((), (), s32[]{:S(2)}) async-start(), calls=%async_computation | async-start | bytes 5242880 | tf_op jit(solution)/shard_map/psum | solution.py:287
  7.2 1.2 copy-start
  8.4 1.4 copy-start.2
  9.8 1.2 copy-start.4
  11.1 1.0 copy-start.5
  12.1 0.7 copy-start.6
  12.8 82.0 %copy-start.1 = (f32[4,256,256]{2,1,0:T(8,128)S(1)}, f32[4,256,256]{2,1,0:T(8,128)}, u32[]{:S(2)}) copy-start(f32[4,256,256]{2,1,0:T(8,128)} %diag_ref.1) | copy-start | bytes 3145732
  12.8 82.0 %copy-start.3 = (f32[6,256,256]{2,1,0:T(8,128)S(1)}, f32[6,256,256]{2,1,0:T(8,128)}, u32[]{:S(2)}) copy-start(f32[6,256,256]{2,1,0:T(8,128)} %win_ref.1) | copy-start | bytes 4718596
  197.5 2.0 copy-start.8
  197.7 1.9 copy-start.9
  199.4 3.1 %slice-start = ((f32[10,256,256]{2,1,0:T(8,128)}), f32[2,256,256]{2,1,0:T(8,128)S(1)}, s32[]{:S(2)}) async-start(f32[10,256,256]{2,1,0:T(8,128)} %all-reduce.3.cloned.1.call-done), calls=%async_computation.1 | async-start | bytes 1048576 | tf_op jit(solution)/shard_map/slice | solution.py:291
  201.0 3.0 %copy-start.7 = (f32[4,256,4,256]{3,2,1,0:T(4,128)S(1)}, f32[4,256,4,256]{3,2,1,0:T(4,128)}, u32[]{:S(2)}) copy-start(f32[4,256,4,256]{3,2,1,0:T(4,128)} %reshape.7) | copy-start | bytes 12582916
Sparse Core Ops, SparseCore 0:
  94.9 99.6 all-reduce.2

commit v2 on v1

--- a/solution.py
+++ b/solution.py
@@ -31,9 +31,19 @@
 
 
 def kernel(
-    n_prow, n_pcol, readers_ref, a_ref, f_ref, win_ref, diag_ref, panels_ref, z_ref,
-    v_ref, whole_ref, part_ref, inbox_ref, g1_send, g1_recv, g2_send, g2_recv, rs_send, rs_recv,
+    n_prow, n_pcol, readers_ref, a_hbm, f_hbm, win_hbm, diag_hbm, panels_ref, window_ref,
+    a_ref, f_ref, win_ref, diag_ref, v_ref, whole_ref, part_ref, inbox_ref, sum_ref, final_ref,
+    line_ref, load_sem, g1_send, g1_recv, g2_send, g2_recv, rs_send, rs_recv,
+    half_send, half_recv, line_send, line_recv, back_send, back_recv, whole_send, whole_recv, *half_refs,
 ):
+    loads = [
+        pltpu.make_async_copy(source, target, load_sem.at[at])
+        for at, (source, target) in enumerate(
+            [(f_hbm, f_ref), (diag_hbm, diag_ref), (win_hbm, win_ref), (a_hbm, a_ref)]
+        )
+    ]
+    for load in loads:
+        load.start()
     count, fine, width = f_ref.shape
     per_column = n_prow // n_pcol
     step = n_prow // PIECES
@@ -58,8 +68,13 @@
     reader = readers_ref[(p * n_pcol + z) * fine // BLK]
     masks = [jnp.where(reader <= node, 1.0, 0.0).astype(jnp.float32) for node in range(count)]
 
+    share = v_ref.shape[1] - fine
+    unit_row = lax.broadcasted_iota(jnp.int32, (share, width), 0) + (p * n_pcol + z) * share
+    unit_col = lax.broadcasted_iota(jnp.int32, (share, width), 1)
+
     def local_v(node):
-        total = f_ref[node] * masks[node]
+        units = jnp.where(unit_row == unit_col + node * width, 1.0, 0.0).astype(jnp.float32)
+        total = jnp.concatenate([f_ref[node] * masks[node], units], axis=0)
         for other in range(node + 1, count):
             total = total - matmul(v_ref[other], win_ref[other * (other - 1) // 2 + node])
         v_ref[node] = matmul(total, diag_ref[node])
@@ -193,107 +208,234 @@
     vt_split = {}
 
     def window_part(node):
-        x = split(-panels_x(node))
+        x = split(jnp.concatenate([part_ref[node, z], v_ref[node, pl.ds(fine, share)]], axis=0))
         for other in range(node + 1):
-            z_ref[pair_at(other, node)] = product(vt_split[other], x)
-
-    def panels_x(node):
-        return -part_ref[node, z]
-
+            sum_ref[pair_at(other, node)] = product(vt_split[other], x)
+
+    bits = len(half_refs)
+    starts = [0]
+    for bit in range(bits):
+        starts.append(starts[bit] + (p // 2**bit) % 2 * (width // 2 ** (bit + 1)))
+    region = width // n_prow
+    full = region // n_pcol % 8 != 0
+    piece = region if full else region // n_pcol
+
+    def blocks(node):
+        return pl.ds(pair_at(0, node), node + 1)
+
+    def rows(start, size):
+        return pl.ds(pl.multiple_of(start, 8), size)
+
+    def partner(bit):
+        return {"prow": p + (1 - (p // 2**bit) % 2 * 2) * 2**bit, "pcol": z}
+
+    def half_copy(node, bit):
+        half = width // 2 ** (bit + 1)
+        away = starts[bit] + (1 - (p // 2**bit) % 2) * half
+        return pltpu.make_async_remote_copy(
+            src_ref=sum_ref.at[blocks(node), rows(away, half)],
+            dst_ref=half_refs[bit].at[blocks(node)],
+            send_sem=half_send.at[node, bit],
+            recv_sem=half_recv.at[node, bit],
+            device_id=partner(bit),
+            device_id_type=MESH,
+        )
+
+    def half_end(node, bit):
+        half_copy(node, bit).wait_recv()
+        mine = rows(starts[bit + 1], width // 2 ** (bit + 1))
+        sum_ref[blocks(node), mine] += half_refs[bit][blocks(node)]
+
+    def piece_rows(dest):
+        return rows(starts[bits] if full else starts[bits] + dest * piece, piece)
+
+    def line_copy(node, dest, source):
+        return pltpu.make_async_remote_copy(
+            src_ref=sum_ref.at[blocks(node), piece_rows(dest)],
+            dst_ref=line_ref.at[source, blocks(node)],
+            send_sem=line_send.at[node, dest],
+            recv_sem=line_recv.at[node, source],
+            device_id={"prow": p, "pcol": dest},
+            device_id_type=MESH,
+        )
+
+    def back_copy(node, dest, source):
+        return pltpu.make_async_remote_copy(
+            src_ref=final_ref.at[blocks(node), piece_rows(source)],
+            dst_ref=final_ref.at[blocks(node), piece_rows(source)],
+            send_sem=back_send.at[node, dest],
+            recv_sem=back_recv.at[node, source],
+            device_id={"prow": p, "pcol": dest},
+            device_id_type=MESH,
+        )
+
+    def others(run):
+        for at in range(n_pcol):
+            @pl.when(z != at)
+            def _():
+                run(at)
+
+    def line_end(node):
+        def add(source):
+            line_copy(node, z, source).wait_recv()
+            sum_ref[blocks(node), piece_rows(z)] += line_ref[source, blocks(node)]
+
+        if full:
+            sum_at = jnp.zeros((node + 1, piece, width), jnp.float32)
+            line_ref[z, blocks(node)] = sum_ref[blocks(node), piece_rows(z)]
+            others(lambda source: line_copy(node, z, source).wait_recv())
+            for source in range(n_pcol):
+                sum_at = sum_at + line_ref[source, blocks(node)]
+            final_ref[blocks(node), piece_rows(z)] = sum_at
+        else:
+            others(add)
+            final_ref[blocks(node), piece_rows(z)] = sum_ref[blocks(node), piece_rows(z)]
+
+    def whole_copy(node, bit, start):
+        part = rows(start, width // 2 ** (bit + 1))
+        return pltpu.make_async_remote_copy(
+            src_ref=final_ref.at[blocks(node), part],
+            dst_ref=final_ref.at[blocks(node), part],
+            send_sem=whole_send.at[node, bit],
+            recv_sem=whole_recv.at[node, bit],
+            device_id=partner(bit),
+            device_id_type=MESH,
+        )
+
+    def whole_start(node, bit):
+        whole_copy(node, bit, starts[bit + 1]).start()
+
+    def whole_end(node, bit):
+        whole_copy(node, bit, starts[bit + 1]).wait_recv()
+
+    def write(node):
+        for other in range(node + 1):
+            block = final_ref[pair_at(other, node)]
+            window_ref[other, node] = block
+            if other < node:
+                window_ref[node, other] = block.T
+
+    def stage(node, at):
+        if at == 0:
+            g2_wait(node)
+            multiply(node)
+            rs_steps(node, False)
+        elif at == 1:
+            rs_steps(node, True)
+        elif at == 2:
+            rs_end(node)
+            window_part(node)
+            half_copy(node, 0).start()
+        elif at < 3 + bits:
+            bit = at - 3
+            half_end(node, bit)
+            if bit + 1 < bits:
+                half_copy(node, bit + 1).start()
+            else:
+                others(lambda dest: line_copy(node, dest, z).start())
+        elif at == 3 + bits:
+            line_end(node)
+            if not full:
+                others(lambda dest: back_copy(node, dest, z).start())
+        elif at == 4 + bits:
+            if not full:
+                others(lambda source: back_copy(node, z, source).wait_recv())
+            whole_start(node, bits - 1)
+        else:
+            bit = 2 * bits + 4 - at
+            whole_end(node, bit)
+            if bit > 0:
+                whole_start(node, bit - 1)
+            else:
+                write(node)
+
+    loads[0].wait()
+    loads[1].wait()
     local_v(order[0])
     pl.semaphore_wait(barrier, n_prow * n_pcol - 1)
     g1_start(order[0])
+    loads[2].wait()
     for node in order[1:]:
         local_v(node)
         g1_start(node)
+    loads[3].wait()
     a_split.append(split(a_ref[...]))
     for node in range(count):
         vt_split[node] = split(v_ref[node].T)
     g2_start(order[0])
-    for at, node in enumerate(order):
-        if at + 1 < count:
-            g2_start(order[at + 1])
-        g2_wait(node)
-        multiply(node)
-        rs_steps(node, False)
-        if at >= 1:
-            rs_steps(order[at - 1], True)
-        if at >= 2:
-            rs_end(order[at - 2])
-            window_part(order[at - 2])
-    rs_steps(order[-1], True)
-    for node in order[max(count - 2, 0):]:
-        rs_end(node)
-        window_part(node)
+    last = 5 + 2 * bits
+    for turn in range(count + last - 1):
+        if turn + 1 < count:
+            g2_start(order[turn + 1])
+        for at in range(last):
+            if 0 <= turn - at < count:
+                stage(order[turn - at], at)
     for node in order:
         g1_finish(node)
         g2_finish(node)
         rs_finish(node)
+        for bit in range(bits):
+            half_copy(node, bit).wait_send()
+            whole_copy(node, bit, starts[bit + 1]).wait_send()
+        others(lambda dest: line_copy(node, dest, z).wait_send())
+        if not full:
+            others(lambda dest: back_copy(node, dest, z).wait_send())
 
 
 def sweep(n_prow, n_pcol, readers, anc_inverse, anc_factor, win_factor, diag_inverse):
     count, fine, width = anc_factor.shape
     pairs = count * (count + 1) // 2
     sources = n_prow // n_pcol * n_pcol
+    share = count * width // (n_prow * n_pcol)
+    bits = n_prow.bit_length() - 1
+    region = width // n_prow
+    piece = region if region // n_pcol % 8 != 0 else region // n_pcol
     vmem = pl.BlockSpec(memory_space=pltpu.VMEM)
+    operands = (anc_inverse, anc_factor, win_factor, diag_inverse)
     return pl.pallas_call(
         functools.partial(kernel, n_prow, n_pcol),
         out_shape=(
             jax.ShapeDtypeStruct((count, fine, width), jnp.float32),
-            jax.ShapeDtypeStruct((pairs, width, width), jnp.float32),
+            jax.ShapeDtypeStruct((count, count, width, width), jnp.float32),
         ),
-        in_specs=[pl.BlockSpec(memory_space=pltpu.SMEM)] + [vmem] * 4,
+        in_specs=[pl.BlockSpec(memory_space=pltpu.SMEM)] + [pl.BlockSpec(memory_space=pltpu.HBM)] * 4,
         out_specs=(vmem, vmem),
-        scratch_shapes=[
-            pltpu.VMEM((count, fine, width), jnp.float32),
+        scratch_shapes=[pltpu.VMEM(operand.shape, jnp.float32) for operand in operands]
+        + [
+            pltpu.VMEM((count, fine + share, width), jnp.float32),
             pltpu.VMEM((count, sources, PIECES, fine // PIECES, width), jnp.float32),
             pltpu.VMEM((count, n_pcol, fine, width), jnp.float32),
             pltpu.VMEM((count, 2, n_pcol, fine, width), jnp.float32),
+            pltpu.VMEM((pairs, width, width), jnp.float32),
+            pltpu.VMEM((pairs, width, width), jnp.float32),
+            pltpu.VMEM((n_pcol, pairs, piece, width), jnp.float32),
+            pltpu.SemaphoreType.DMA((len(operands),)),
             pltpu.SemaphoreType.DMA((count, PIECES)),
             pltpu.SemaphoreType.DMA((count,)),
             pltpu.SemaphoreType.DMA((count, n_prow)),
             pltpu.SemaphoreType.DMA((count, PIECES)),
             pltpu.SemaphoreType.DMA((count, n_pcol)),
             pltpu.SemaphoreType.DMA((count, 2, n_pcol)),
-        ],
+            pltpu.SemaphoreType.DMA((count, bits)),
+            pltpu.SemaphoreType.DMA((count, bits)),
+            pltpu.SemaphoreType.DMA((count, n_pcol)),
+            pltpu.SemaphoreType.DMA((count, n_pcol)),
+            pltpu.SemaphoreType.DMA((count, n_pcol)),
+            pltpu.SemaphoreType.DMA((count, n_pcol)),
+            pltpu.SemaphoreType.DMA((count, bits)),
+            pltpu.SemaphoreType.DMA((count, bits)),
+        ]
+        + [pltpu.VMEM((pairs, width // 2 ** (bit + 1), width), jnp.float32) for bit in range(bits)],
         compiler_params=pltpu.CompilerParams(
-            collective_id=0, has_side_effects=True, vmem_limit_bytes=48 * 2**20
+            collective_id=0, has_side_effects=True, vmem_limit_bytes=56 * 2**20
         ),
-    )(readers, anc_inverse, anc_factor, win_factor, diag_inverse)
-
-
-def window_own(win_factor, diag_inverse):
-    dot = functools.partial(jnp.dot, precision=lax.Precision.HIGH)
-    count, width, _ = diag_inverse.shape
-    columns = []
-    for node in range(count):
-        column = [jnp.zeros((width, width), jnp.float32)] * node + [diag_inverse[node]]
-        for row in range(node + 1, count):
-            total = sum(dot(win_factor[row * (row - 1) // 2 + at], column[at]) for at in range(node, row))
-            column.append(-dot(diag_inverse[row], total))
-        columns.append(jnp.concatenate(column, axis=0))
-    whole = jnp.concatenate(columns, axis=1)
-    return dot(whole.T, whole)
+    )(readers, *operands)
 
 
 def per_device(anc_inverse, anc_factor, win_factor, diag_inverse, first_reader):
     n_prow = lax.axis_size("prow")
     n_pcol = lax.axis_size("pcol")
-    count, _, width = anc_factor.shape
-    panels, partial = sweep(
-        n_prow, n_pcol, first_reader, anc_inverse, anc_factor, win_factor, diag_inverse
-    )
-    own = window_own(win_factor, diag_inverse)
-    summed = lax.psum(partial, ("prow", "pcol"))
-    own = own.reshape(count, width, count, width).transpose(0, 2, 1, 3)
-    cross = jnp.stack([
-        jnp.stack([
-            summed[pair_at(row, col)] if row <= col else summed[pair_at(col, row)].T
-            for col in range(count)
-        ])
-        for row in range(count)
-    ])
-    return panels, own + cross
+    return sweep(n_prow, n_pcol, first_reader, anc_inverse, anc_factor, win_factor, diag_inverse)
 
 
 def solution(mesh):

time: 215 us -> 122 us (0.57)
  waiting for transfers between devices: 78.8 us -> 0 us
  Pallas kernels: 82 us -> 114 us
  matrix products: 15.1 us -> 0 us
  between operations: 14.3 us -> 0.64 us
  local copies, waits for them, and re-layouts: 17.4 us -> 6.46 us
  other arithmetic: 7.05 us -> 0 us
    psum x1 -> x0, waiting for transfers between devices: 78.7 us -> none  [per_device(): summed = lax.psum(partial, ('prow', 'pcol'))]
    pallas_call x1, Pallas kernels: 82 us -> 114 us  [sweep(): pl.pallas_call(functools.partial(kernel, n_prow, n_pcol), out_shape=(jax....]
    dot_general x17 -> x0, matrix products: 15.1 us -> none  [the longest x1 10 us: window_own(): return dot(whole.T, whole)]
    reshape x1 -> x0, local copies, waits for them, and re-layouts: 5.67 us -> none  [per_device(): own = own.reshape(count, width, count, width).transpose(0, 2, 1, 3)]
    another operation x3 -> x0, other arithmetic: 3.97 us -> none  [per_device(): jnp.stack([jnp.stack([summed[pair_at(row, col)] if row <= col else summed...]
    add x1 -> x0, other arithmetic: 3.08 us -> none  [per_device(): return (panels, own + cross)]
    slice x3 -> x0, local copies, waits for them, and re-layouts: 2.74 us -> none  [per_device(): summed[pair_at(row, col)]]
    unnamed x25 -> x2, local copies, waits for them, and re-layouts: 6.87 us -> 6.46 us
  transfers between devices with their start and end apart: 1 -> 0, of which waited for: 1 -> 0; matrix products, arithmetic and copies ran while one was open for 10% -> 0% of each run, Pallas kernels for 0% -> 0%
where the time goes in v2:
time: 122 us
  Pallas kernels  114 us (93%)
  local copies, waits for them, and re-layouts  6.46 us (5%)
    pallas_call x1, Pallas kernels, sweep(): pl.pallas_call(functools.partial(kernel, n_prow, n_pcol), out_shape=(jax....  114 us
    unnamed x2, local copies, waits for them, and re-layouts  6.46 us

profile of v2, /device:TPU:0, one launch (start us, length us, event | category | flops | bytes accessed | tf_op | source)
XLA Modules:
  0.0 121.6 jit_solution(14184734638799130721)
XLA Ops:
  0.6 114.5 %shard_map.68 = (f32[4,128,256]{2,1,0:T(8,128)}, f32[4,4,256,256]{3,2,1,0:T(8,128)}) custom-call(s32[16]{0:T(128)} %readers_ref.1, f32[512,512]{1,0:T(8,128)} %a_hbm.1, f32[4,128,256]{2,1,0:T(8,128)} %f_hbm.1, f32[6,256,256]{2,1,0:T(8,128)} %win_hbm.1, f32[4,256,256]{2,1,0:T(8,128)} %diag_hbm.1), custom_call_target="tpu_custom_call" | custom-call | tf_op jit(solution)/shard_map/pallas_call | solution.py:395
  115.1 1.9 %copy.9 = f32[4,128,256]{2,1,0:T(8,128)} copy(f32[4,128,256]{2,1,0:T(8,128)} %get-tuple-element.4) | data formatting | bytes 1048576
  117.0 4.6 %copy.10 = f32[4,4,256,256]{3,2,1,0:T(8,128)} copy(f32[4,4,256,256]{3,2,1,0:T(8,128)} %get-tuple-element.5) | data formatting | bytes 8388608

commit v3 on v2

--- a/solution.py
+++ b/solution.py
@@ -427,7 +427,7 @@
         ]
         + [pltpu.VMEM((pairs, width // 2 ** (bit + 1), width), jnp.float32) for bit in range(bits)],
         compiler_params=pltpu.CompilerParams(
-            collective_id=0, has_side_effects=True, vmem_limit_bytes=56 * 2**20
+            collective_id=0, has_side_effects=True, vmem_limit_bytes=40 * 2**20
         ),
     )(readers, *operands)
 

time: 122 us -> 122 us (level)
  Pallas kernels: 114 us -> 112 us
  local copies, waits for them, and re-layouts: 6.46 us -> 8.35 us
    pallas_call x1, Pallas kernels: 114 us -> 112 us  [sweep(): pl.pallas_call(functools.partial(kernel, n_prow, n_pcol), out_shape=(jax....]
    unnamed x2 -> x12, local copies, waits for them, and re-layouts: 6.46 us -> 8.35 us
where the time goes in v3:
time: 122 us; the launch traced here: 121 us
  Pallas kernels  112 us (92%)
  local copies, waits for them, and re-layouts  8.35 us (7%)
    pallas_call x1, Pallas kernels, sweep(): pl.pallas_call(functools.partial(kernel, n_prow, n_pcol), out_shape=(jax....  112 us
    unnamed x12, local copies, waits for them, and re-layouts  8.35 us

profile of v3, /device:TPU:0, one launch (start us, length us, event | category | flops | bytes accessed | tf_op | source)
XLA Modules:
  0.0 121.5 jit_solution(6532221798949473682)
XLA Ops:
  0.6 0.0 copy-start
  0.6 1.4 %copy-done = f32[6,256,256]{2,1,0:T(8,128)S(1)} copy-done((f32[6,256,256]{2,1,0:T(8,128)S(1)}, f32[6,256,256]{2,1,0:T(8,128)}, u32[]{:S(2)}) %copy-start) | copy-done | bytes 1572888
  2.0 0.0 copy-start.1
  2.0 1.2 %copy-done.1 = f32[512,512]{1,0:T(8,128)S(1)} copy-done((f32[512,512]{1,0:T(8,128)S(1)}, f32[512,512]{1,0:T(8,128)}, u32[]{:S(2)}) %copy-start.1) | copy-done | bytes 1048600
  3.3 0.0 copy-start.2
  3.3 1.2 %copy-done.2 = f32[4,256,256]{2,1,0:T(8,128)S(1)} copy-done((f32[4,256,256]{2,1,0:T(8,128)S(1)}, f32[4,256,256]{2,1,0:T(8,128)}, u32[]{:S(2)}) %copy-start.2) | copy-done | bytes 1048600
  4.5 0.0 copy-start.3
  4.5 1.0 copy-done.3
  5.5 0.0 copy-start.4
  5.5 0.7 copy-done.4
  6.2 112.5 %shard_map.68 = (f32[4,128,256]{2,1,0:T(8,128)S(1)}, f32[4,4,256,256]{3,2,1,0:T(8,128)S(1)}) custom-call(s32[16]{0:T(128)S(1)} %copy-done.4, f32[512,512]{1,0:T(8,128)S(1)} %copy-done.1, f32[4,128,256]{2,1,0:T(8,128)S(1)} %copy-done.3, f32[6,256,256]{2,1,0:T(8,128)S(1)} %copy-done, f32[4,256,256]{2,1,0:T(8,128)S(1)} %copy-done.2), custom_call_target="tpu_custom_call" | custom-call | tf_op jit(solution)/shard_map/pallas_call | solution.py:395
  118.7 0.8 copy.9
  119.5 2.0 %copy.10 = f32[4,4,256,256]{3,2,1,0:T(8,128)} copy(f32[4,4,256,256]{3,2,1,0:T(8,128)S(1)} %get-tuple-element.5) | data formatting | bytes 8388608
Async XLA Ops:
  0.6 1.4 %copy-start = (f32[6,256,256]{2,1,0:T(8,128)S(1)}, f32[6,256,256]{2,1,0:T(8,128)}, u32[]{:S(2)}) copy-start(f32[6,256,256]{2,1,0:T(8,128)} %win_hbm.1) | copy-start | bytes 4718596
  2.0 1.2 %copy-start.1 = (f32[512,512]{1,0:T(8,128)S(1)}, f32[512,512]{1,0:T(8,128)}, u32[]{:S(2)}) copy-start(f32[512,512]{1,0:T(8,128)} %a_hbm.1) | copy-start | bytes 3145732
  3.3 1.2 %copy-start.2 = (f32[4,256,256]{2,1,0:T(8,128)S(1)}, f32[4,256,256]{2,1,0:T(8,128)}, u32[]{:S(2)}) copy-start(f32[4,256,256]{2,1,0:T(8,128)} %diag_hbm.1) | copy-start | bytes 3145732
  4.5 1.0 copy-start.3
  5.5 0.7 copy-start.4
